TPU v7x, 32 devices: a whole 2x2x4 slice. The times are simulated.
32 devices in a mesh: pipe: 2 (over x), dom: 8 (over z, y), rep: 2 (over core).
Axes of the slice: x: 2, y: 2, z: 4, core: 2. Of those that a mesh axis runs over, the one named last changes fastest.
Arguments:
- handoff: bfloat16 [2, 2, 4096, 512], P('pipe', 'rep', 'dom'), may hold values from -6 to 6
- initial: bfloat16 [2, 2, 4096, 512], P('pipe', 'rep', 'dom'), may hold values from -6 to 6
- cotangent: bfloat16 [2, 2, 4096, 512], P('pipe', 'rep', 'dom'), may hold values from -6 to 6
- slots: int32 [2, 2, 4096, 16], P('pipe', 'rep', 'dom'), may hold values from 0 to 639
- edge_weight: bfloat16 [2, 2, 4096, 16], P('pipe', 'rep', 'dom'), may hold values from 0.029907227 to 0.119628906
- boundary: int32 [2, 2, 8, 2, 64], P('pipe', 'rep', 'dom'), may hold values from 0 to 511
- weights: bfloat16 [4, 512, 512], P('pipe'), may hold values from -0.25 to 0.25
Outputs:
- section_out: bfloat16 [2, 2, 4096, 512], P('pipe', 'rep', 'dom')
- input_grad: bfloat16 [2, 2, 4096, 512], P('pipe', 'rep', 'dom')
- weight_grad: bfloat16 [4, 512, 512], P('pipe')
All inputs are finite; a program needn't handle non-finite values.
Results may differ from a plain program's by a relative error of at most 0.013.
Values may be sent and summed in bfloat16 or wider, within the bound.
A program may use at most 64 MiB of HBM per device.

v0:
```python
import math

import jax
import jax.numpy as jnp
from jax import lax
from jax.sharding import PartitionSpec as P

ALPHA = 0.1


def passed_along(shard, axis, by):
    peers = lax.axis_size(axis)
    return lax.ppermute(shard, axis, [(i, (i + by) % peers) for i in range(peers)])


def adjacency(slot_rows, weight_rows, width):
    columns = jnp.arange(width, dtype=jnp.int32)
    total = jnp.zeros((slot_rows.shape[0], width), jnp.float32)
    for k in range(slot_rows.shape[1]):
        total = total + jnp.where(
            slot_rows[:, k][:, None] == columns[None, :],
            weight_rows[:, k][:, None].astype(jnp.float32),
            jnp.float32(0.0),
        )
    return total.astype(jnp.bfloat16)


def silu_slope(value):
    sig = jax.nn.sigmoid(value)
    return sig * (1.0 + value * (1.0 - sig))


def extend(rows, bound):
    to_prev = rows[bound[0]]
    to_next = rows[bound[1]]
    from_prev = passed_along(to_next, "dom", 1)
    from_next = passed_along(to_prev, "dom", -1)
    return jnp.concatenate([from_prev, rows, from_next], axis=0)


def retract(dext, bound, rows, width):
    own = dext[width : width + rows]
    back_prev = dext[:width]
    back_next = dext[width + rows :]
    from_next = passed_along(back_prev, "dom", -1)
    from_prev = passed_along(back_next, "dom", 1)
    return own.at[bound[0]].add(from_prev).at[bound[1]].add(from_next)


def local(handoff, initial, cotangent, slots, edge_weight, boundary, weights):
    f32 = jnp.float32
    rows = handoff.shape[2]
    width = boundary.shape[-1]
    layers = weights.shape[0]
    scale = 1.0 / math.sqrt(rows * lax.axis_size("dom") * lax.axis_size("rep"))
    segment = lax.axis_index("pipe")
    betas = [
        jnp.log(0.5 / (segment * layers + layer + 1).astype(f32) + 1.0) for layer in range(layers)
    ]
    state = passed_along(handoff[0, 0], "pipe", 1)
    start = initial[0, 0].astype(f32)
    adj = adjacency(slots[0, 0], edge_weight[0, 0], rows + 2 * width)
    bound = boundary[0, 0, 0]
    saved = []
    for layer in range(layers):
        beta = betas[layer]
        ext = extend(state, bound)
        agg = jnp.dot(adj, ext, preferred_element_type=f32)
        s_act = ((1.0 - ALPHA) * agg + ALPHA * start).astype(jnp.bfloat16)
        mixed = jnp.dot(s_act, weights[layer], preferred_element_type=f32)
        z_val = (1.0 - beta) * s_act.astype(f32) + beta * mixed
        state = jax.nn.silu(z_val).astype(jnp.bfloat16)
        saved.append((s_act, z_val))
    grad = passed_along(cotangent[0, 0], "pipe", -1)
    finished = [None] * layers
    for layer in reversed(range(layers)):
        beta = betas[layer]
        s_act, z_val = saved[layer]
        dz_val = (grad.astype(f32) * silu_slope(z_val)).astype(jnp.bfloat16)
        term = lax.dot_general(s_act, dz_val, (((0,), (0,)), ((), ())), preferred_element_type=f32)
        summed = lax.psum(term, ("dom", "rep"))
        finished[layer] = (beta * scale * summed).astype(jnp.bfloat16)
        back = lax.dot_general(
            dz_val, weights[layer], (((1,), (1,)), ((), ())), preferred_element_type=f32
        )
        ds_val = (1.0 - beta) * dz_val.astype(f32) + beta * back
        dagg = ((1.0 - ALPHA) * ds_val).astype(jnp.bfloat16)
        dext = lax.dot_general(adj, dagg, (((0,), (0,)), ((), ())), preferred_element_type=f32)
        grad = retract(dext, bound, rows, width).astype(jnp.bfloat16)
    weight_grad = jnp.stack(finished)
    return (state[None, None], grad[None, None], weight_grad)


def solution(mesh):
    in_specs = (
        P("pipe", "rep", "dom", None),
        P("pipe", "rep", "dom", None),
        P("pipe", "rep", "dom", None),
        P("pipe", "rep", "dom", None),
        P("pipe", "rep", "dom", None),
        P("pipe", "rep", "dom", None, None),
        P("pipe", None, None),
    )
    out_specs = (
        P("pipe", "rep", "dom", None),
        P("pipe", "rep", "dom", None),
        P("pipe", None, None),
    )
    return jax.shard_map(local, mesh=mesh, in_specs=in_specs, out_specs=out_specs, check_vma=False)
```

profile of v0, /device:TPU:1, one launch (start us, length us, event | category | flops | bytes accessed | tf_op | source)
XLA Modules:
  0.0 185.8 jit_solution(13704241570418847226)
XLA Ops:
  7.2 0.0 all-reduce.3.cloned.1.call-start
  7.2 2.1 %collective-permute-start.5 = (bf16[512,512]{1,0:T(8,128)(2,1)}, bf16[512,512]{1,0:T(8,128)(2,1)}, u32[]{:S(2)}, u32[]{:S(2)}) collective-permute-start(bf16[512,512]{1,0:T(8,128)(2,1)} %bitcast.118), channel_id=1, source_target_pairs={{0,16},{16,0},{1,17},{17,1},{2,18},{18,2},{3,19},{19,3},{4,20},{20... | collective-permute-start | bytes 1572872 | tf_op jit(solution)/shard_map/ppermute | solution.py:13
  9.3 0.1 collective-permute-start
  9.4 0.8 fusion.44
  10.2 1.0 slice_convert_fusion.15
  11.2 1.1 fusion.52
  12.3 20.1 %collective-permute-done = bf16[512,512]{1,0:T(8,128)(2,1)S(1)} collective-permute-done((bf16[512,512]{1,0:T(8,128)(2,1)}, bf16[512,512]{1,0:T(8,128)(2,1)S(1)}, u32[]{:S(2)}, u32[]{:S(2)}) %collective-permute-start) | collective-permute-done | bytes 524320 | tf_op jit(solution)/shard_map/ppermute | solution.py:13
  32.4 0.7 gather_fusion.1
  33.1 4.3 %collective-permute-start.2 = (bf16[64,512]{1,0:T(8,128)(2,1)S(1)}, bf16[64,512]{1,0:T(8,128)(2,1)S(1)}, u32[]{:S(2)}, u32[]{:S(2)}) collective-permute-start(bf16[64,512]{1,0:T(8,128)(2,1)S(1)} %gather_fusion.1), channel_id=1, source_target_pairs={{0,14},{2,0},{4,2},{6,4},{8,6},{10,8},{12,10},{14,12},{1,15},{3,1}... | collective-permute-start | bytes 196616 | tf_op jit(solution)/shard_map/ppermute | solution.py:13
  37.4 0.7 gather_fusion
  38.1 0.1 collective-permute-start.1
  38.2 2.9 %add_convert_fusion = bf16[512,640]{1,0:T(8,128)(2,1)S(1)} fusion(f32[512]{0:T(512)S(1)} %bitcast.86, s32[512]{0:T(512)S(1)} %bitcast.102, f32[512]{0:T(512)S(1)} %bitcast.87, s32[512]{0:T(512)S(1)} %bitcast.103, f32[512]{0:T(512)S(1)} %bitcast.88, s32[512]{0:T(512)S(1)} %bitcast.104, f32[512]{0:T(512)S(1)} %bitcast.89, s32[512]{0:T(512)S(1)} %bitcast.105, ...), kind=kLoop, calls=%fused_computation.20 | loop fusion | flops 15728640 | bytes 720896 | tf_op jit(solution)/shard_map/convert_element_type | solution.py:25
  41.2 0.0 copy-start.6
  41.2 2.7 %collective-permute-done.1 = bf16[64,512]{1,0:T(8,128)(2,1)S(1)} collective-permute-done((bf16[64,512]{1,0:T(8,128)(2,1)S(1)}, bf16[64,512]{1,0:T(8,128)(2,1)S(1)}, u32[]{:S(2)}, u32[]{:S(2)}) %collective-permute-start.1) | collective-permute-done | bytes 65568 | tf_op jit(solution)/shard_map/ppermute | solution.py:13
  44.0 0.6 fusion.6
  44.6 0.6 multiply_convert_fusion.6
  45.2 0.1 copy-done.3
  45.3 0.7 gather_fusion.3
  46.0 0.7 gather_fusion.2
  46.7 2.2 %collective-permute-start.4 = (bf16[64,512]{1,0:T(8,128)(2,1)S(1)}, bf16[64,512]{1,0:T(8,128)(2,1)S(1)}, u32[]{:S(2)}, u32[]{:S(2)}) collective-permute-start(bf16[64,512]{1,0:T(8,128)(2,1)S(1)} %gather_fusion.3), channel_id=1, source_target_pairs={{0,14},{2,0},{4,2},{6,4},{8,6},{10,8},{12,10},{14,12},{1,15},{3,1}... | collective-permute-start | bytes 196616 | tf_op jit(solution)/shard_map/ppermute | solution.py:13
  49.0 0.0 copy-start.7
  49.0 1.2 collective-permute-done.4
  50.2 4.5 %collective-permute-done.3 = bf16[64,512]{1,0:T(8,128)(2,1)S(1)} collective-permute-done((bf16[64,512]{1,0:T(8,128)(2,1)S(1)}, bf16[64,512]{1,0:T(8,128)(2,1)S(1)}, u32[]{:S(2)}, u32[]{:S(2)}) %collective-permute-start.3) | collective-permute-done | bytes 65568 | tf_op jit(solution)/shard_map/ppermute | solution.py:13
  54.7 0.6 fusion.7
  55.3 3.1 %multiply_convert_fusion.4 = (bf16[512,512]{1,0:T(8,128)(2,1)}, bf16[1,1,512,512]{3,2,1,0:T(8,128)(2,1)}) fusion(bf16[512,512]{1,0:T(8,128)(2,1)} %collective-permute-done.5, bf16[512,512]{1,0:T(8,128)(2,1)S(1)} %fusion.7, bf16[2,512,512]{2,1,0:T(8,128)(2,1)S(1)} %copy-done.7, f32[]{:T(128)S(6)} %log.6, f32[]{:T(128)S(6)} %sub.14), kind=kOutput, calls=%fused_computation.48 | convolution fusion | flops 272629760 | bytes 3145736 | tf_op jit(solution)/shard_map/dot_general | solution.py:70
  58.4 2.2 %fusion.22 = f32[640,512]{1,0:T(8,128)S(1)} fusion(bf16[512,640]{1,0:T(8,128)(2,1)S(1)} %copy-done.1, bf16[512,512]{1,0:T(8,128)(2,1)} %get-tuple-element.9, f32[]{:T(128)S(6)} %log.6, f32[]{:T(128)S(6)} %sub.14, bf16[2,512,512]{2,1,0:T(8,128)(2,1)} %param.13), kind=kOutput, calls=%fused_computation.64 | convolution fusion | flops 605552640 | bytes 3538952 | tf_op jit(solution)/shard_map/dot_general | solution.py:88
  60.7 0.7 fusion.51
  61.3 4.2 %collective-permute-start.7 = (f32[64,512]{1,0:T(8,128)}, f32[64,512]{1,0:T(8,128)S(1)}, u32[]{:S(2)}, u32[]{:S(2)}) collective-permute-start(f32[64,512]{1,0:T(8,128)} %get-tuple-element.7), channel_id=1, source_target_pairs={{0,14},{2,0},{4,2},{6,4},{8,6},{10,8},{12,10},{14,12},{1,15},{3,1}... | collective-permute-start | bytes 393224 | tf_op jit(solution)/shard_map/ppermute | solution.py:13
  65.5 2.6 %fusion.56 = f32[512,512]{1,0:T(8,128)} fusion(bf16[512,512]{1,0:T(8,128)(2,1)} %copy-done.5, bf16[512,512]{1,0:T(8,128)(2,1)} %get-tuple-element.9), kind=kOutput, calls=%fused_computation.113 | convolution fusion | flops 268435456 | bytes 2097152 | tf_op jit(solution)/shard_map/dot_general | solution.py:80
  68.1 0.1 slice.218
  68.2 1.7 scatter_fusion
  70.0 1.4 scatter_fusion.1
  71.4 0.4 multiply_convert_fusion.2
  71.8 0.6 copy-done.4
  72.4 1.4 fusion.55
  73.8 0.0 all-reduce.3.cloned.1.call-update
  73.8 1.1 copy-done.2
  74.9 1.9 %fusion.9 = f32[640,512]{1,0:T(8,128)S(1)} fusion(bf16[512,640]{1,0:T(8,128)(2,1)S(1)} %copy-done.2, bf16[512,512]{1,0:T(8,128)(2,1)S(1)} %multiply_convert_fusion.2, f32[]{:T(128)S(6)} %log.7, f32[]{:T(128)S(6)} %sub.15, bf16[2,512,512]{2,1,0:T(8,128)(2,1)} %param.13), kind=kOutput, calls=%fused_computation.40 | convolution fusion | flops 605552640 | bytes 3538952 | tf_op jit(solution)/shard_map/dot_general | solution.py:88
  76.9 0.1 collective-permute-start.8
  76.9 4.1 %collective-permute-start.9 = (f32[64,512]{1,0:T(8,128)S(1)}, f32[64,512]{1,0:T(8,128)S(1)}, u32[]{:S(2)}, u32[]{:S(2)}) collective-permute-start(f32[64,512]{1,0:T(8,128)S(1)} %get-tuple-element.5), channel_id=1, source_target_pairs={{0,14},{2,0},{4,2},{6,4},{8,6},{10,8},{12,10},{14,12},{1,15},{3,1}... | collective-permute-start | bytes 393224 | tf_op jit(solution)/shard_map/ppermute | solution.py:13
  81.1 0.1 slice.221
  81.2 2.3 %collective-permute-done.8 = f32[64,512]{1,0:T(8,128)S(1)} collective-permute-done((f32[64,512]{1,0:T(8,128)S(1)}, f32[64,512]{1,0:T(8,128)S(1)}, u32[]{:S(2)}, u32[]{:S(2)}) %collective-permute-start.8) | collective-permute-done | bytes 131104 | tf_op jit(solution)/shard_map/ppermute | solution.py:13
  83.4 1.4 scatter_fusion.2
  84.8 1.4 scatter_fusion.3
  86.2 0.9 convert_bitcast_fusion
  87.1 89.1 %all-reduce.3.cloned.1.call-done = (f32[512,512]{1,0:T(8,128)}, f32[512,512]{1,0:T(8,128)}) async-done(((f32[512,512]{1,0:T(8,128)}, f32[512,512]{1,0:T(8,128)}), (f32[512,512]{1,0:T(8,128)}, f32[512,512]{1,0:T(8,128)})) %all-reduce.3.cloned.1.call-update) | async-done | bytes 2097168 | tf_op jit(solution)/shard_map/psum | solution.py:81
  176.1 1.8 fusion.23
  177.9 1.1 pad_maximum_fusion
  (23 shorter events, 0.1 us)
Async XLA Ops:
  7.2 36.8 %copy-start.8 = (bf16[1,1,512,512]{3,2,1,0:T(8,128)(2,1)S(1)}, bf16[1,1,512,512]{3,2,1,0:T(8,128)(2,1)}, u32[]{:S(2)}) copy-start(bf16[1,1,512,512]{3,2,1,0:T(8,128)(2,1)} %param.8) | copy-start | bytes 1572868
  7.2 168.9 %all-reduce.3.cloned.1.call-start = ((), (), s32[]{:S(2)}) async-start(), calls=%async_computation | async-start | bytes 4194304 | tf_op jit(solution)/shard_map/psum | solution.py:81
  7.2 48.1 %collective-permute-start.5 = (bf16[512,512]{1,0:T(8,128)(2,1)}, bf16[512,512]{1,0:T(8,128)(2,1)}, u32[]{:S(2)}, u32[]{:S(2)}) collective-permute-start(bf16[512,512]{1,0:T(8,128)(2,1)} %bitcast.118), channel_id=1, source_target_pairs={{0,16},{16,0},{1,17},{17,1},{2,18},{18,2},{3,19},{19,3},{4,20},{20... | collective-permute-start | bytes 1572872 | tf_op jit(solution)/shard_map/ppermute | solution.py:13
  9.3 23.1 %collective-permute-start = (bf16[512,512]{1,0:T(8,128)(2,1)}, bf16[512,512]{1,0:T(8,128)(2,1)S(1)}, u32[]{:S(2)}, u32[]{:S(2)}) collective-permute-start(bf16[512,512]{1,0:T(8,128)(2,1)} %bitcast.117), channel_id=1, source_target_pairs={{0,16},{16,0},{1,17},{17,1},{2,18},{18,2},{3,19},{19,3},{4,20},{20... | collective-permute-start | bytes 1572872 | tf_op jit(solution)/shard_map/ppermute | solution.py:13
  33.1 8.1 %collective-permute-start.2 = (bf16[64,512]{1,0:T(8,128)(2,1)S(1)}, bf16[64,512]{1,0:T(8,128)(2,1)S(1)}, u32[]{:S(2)}, u32[]{:S(2)}) collective-permute-start(bf16[64,512]{1,0:T(8,128)(2,1)S(1)} %gather_fusion.1), channel_id=1, source_target_pairs={{0,14},{2,0},{4,2},{6,4},{8,6},{10,8},{12,10},{14,12},{1,15},{3,1}... | collective-permute-start | bytes 196616 | tf_op jit(solution)/shard_map/ppermute | solution.py:13
  38.1 5.9 %collective-permute-start.1 = (bf16[64,512]{1,0:T(8,128)(2,1)S(1)}, bf16[64,512]{1,0:T(8,128)(2,1)S(1)}, u32[]{:S(2)}, u32[]{:S(2)}) collective-permute-start(bf16[64,512]{1,0:T(8,128)(2,1)S(1)} %gather_fusion), channel_id=1, source_target_pairs={{0,2},{2,4},{4,6},{6,8},{8,10},{10,12},{12,14},{14,0},{1,3},{3,5},... | collective-permute-start | bytes 196616 | tf_op jit(solution)/shard_map/ppermute | solution.py:13
  41.1 13.6 %copy-start = (bf16[512,640]{1,0:T(8,128)(2,1)}, bf16[512,640]{1,0:T(8,128)(2,1)S(1)}, u32[]{:S(2)}) copy-start(bf16[512,640]{1,0:T(8,128)(2,1)S(1)} %add_convert_fusion) | copy-start | bytes 1966084
  41.2 3.3 %copy-start.6 = (bf16[2,512,512]{2,1,0:T(8,128)(2,1)S(1)}, bf16[2,512,512]{2,1,0:T(8,128)(2,1)}, u32[]{:S(2)}) copy-start(bf16[2,512,512]{2,1,0:T(8,128)(2,1)} %param.13) | copy-start | bytes 3145732
  44.5 0.8 copy-start.3
  46.7 3.5 %collective-permute-start.4 = (bf16[64,512]{1,0:T(8,128)(2,1)S(1)}, bf16[64,512]{1,0:T(8,128)(2,1)S(1)}, u32[]{:S(2)}, u32[]{:S(2)}) collective-permute-start(bf16[64,512]{1,0:T(8,128)(2,1)S(1)} %gather_fusion.3), channel_id=1, source_target_pairs={{0,14},{2,0},{4,2},{6,4},{8,6},{10,8},{12,10},{14,12},{1,15},{3,1}... | collective-permute-start | bytes 196616 | tf_op jit(solution)/shard_map/ppermute | solution.py:13
  48.9 5.8 %collective-permute-start.3 = (bf16[64,512]{1,0:T(8,128)(2,1)S(1)}, bf16[64,512]{1,0:T(8,128)(2,1)S(1)}, u32[]{:S(2)}, u32[]{:S(2)}) collective-permute-start(bf16[64,512]{1,0:T(8,128)(2,1)S(1)} %gather_fusion.2), channel_id=1, source_target_pairs={{0,2},{2,4},{4,6},{6,8},{8,10},{10,12},{12,14},{14,0},{1,3},{3,5},... | collective-permute-start | bytes 196616 | tf_op jit(solution)/shard_map/ppermute | solution.py:13
  49.0 6.3 %copy-start.7 = (bf16[2,512,512]{2,1,0:T(8,128)(2,1)S(1)}, bf16[2,512,512]{2,1,0:T(8,128)(2,1)}, u32[]{:S(2)}) copy-start(bf16[2,512,512]{2,1,0:T(8,128)(2,1)} %param.13) | copy-start | bytes 3145732
  55.3 3.1 %copy-start.5 = (bf16[512,512]{1,0:T(8,128)(2,1)}, bf16[512,512]{1,0:T(8,128)(2,1)S(1)}, u32[]{:S(2)}) copy-start(bf16[512,512]{1,0:T(8,128)(2,1)S(1)} %fusion.7) | copy-start | bytes 1572868
  55.3 3.1 %copy-start.1 = (bf16[512,640]{1,0:T(8,128)(2,1)S(1)}, bf16[512,640]{1,0:T(8,128)(2,1)}, u32[]{:S(2)}) copy-start(bf16[512,640]{1,0:T(8,128)(2,1)} %copy-done) | copy-start | bytes 1966084
  61.3 6.9 %collective-permute-start.6 = (f32[64,512]{1,0:T(8,128)S(1)}, f32[64,512]{1,0:T(8,128)}, u32[]{:S(2)}, u32[]{:S(2)}) collective-permute-start(f32[64,512]{1,0:T(8,128)S(1)} %get-tuple-element.8), channel_id=1, source_target_pairs={{0,2},{2,4},{4,6},{6,8},{8,10},{10,12},{12,14},{14,0},{1,3},{3,5},... | collective-permute-start | bytes 393224 | tf_op jit(solution)/shard_map/ppermute | solution.py:13
  61.3 8.6 %collective-permute-start.7 = (f32[64,512]{1,0:T(8,128)}, f32[64,512]{1,0:T(8,128)S(1)}, u32[]{:S(2)}, u32[]{:S(2)}) collective-permute-start(f32[64,512]{1,0:T(8,128)} %get-tuple-element.7), channel_id=1, source_target_pairs={{0,14},{2,0},{4,2},{6,4},{8,6},{10,8},{12,10},{14,12},{1,15},{3,1}... | collective-permute-start | bytes 393224 | tf_op jit(solution)/shard_map/ppermute | solution.py:13
  71.4 1.0 copy-start.4
  73.8 1.1 copy-start.2
  76.9 6.6 %collective-permute-start.8 = (f32[64,512]{1,0:T(8,128)S(1)}, f32[64,512]{1,0:T(8,128)S(1)}, u32[]{:S(2)}, u32[]{:S(2)}) collective-permute-start(f32[64,512]{1,0:T(8,128)S(1)} %get-tuple-element.6), channel_id=1, source_target_pairs={{0,2},{2,4},{4,6},{6,8},{8,10},{10,12},{12,14},{14,0},{1,3},{3,5},... | collective-permute-start | bytes 393224 | tf_op jit(solution)/shard_map/ppermute | solution.py:13
  76.9 7.9 %collective-permute-start.9 = (f32[64,512]{1,0:T(8,128)S(1)}, f32[64,512]{1,0:T(8,128)S(1)}, u32[]{:S(2)}, u32[]{:S(2)}) collective-permute-start(f32[64,512]{1,0:T(8,128)S(1)} %get-tuple-element.5), channel_id=1, source_target_pairs={{0,14},{2,0},{4,2},{6,4},{8,6},{10,8},{12,10},{14,12},{1,15},{3,1}... | collective-permute-start | bytes 393224 | tf_op jit(solution)/shard_map/ppermute | solution.py:13
Sparse Core Ops, SparseCore 0:
  74.0 102.0 all-reduce.2
where the time goes:
time: 188 us; the launch traced here: 186 us
  waiting for transfers between devices  120 us (64%)
  starting transfers between devices  17.1 us (9%)
  other arithmetic  14.7 us (8%)
  between operations  14.5 us (8%)
  matrix products  13.1 us (7%)
  local copies, waits for them, and re-layouts  6.55 us (3%)
    psum x1, waiting for transfers between devices, local(): summed = lax.psum(term, ('dom', 'rep'))  89.1 us
    ppermute x10, waiting for transfers between devices, passed_along(): lax.ppermute(shard, axis, [(i, (i + by) % peers) for i in range(peers)])  30.9 us
    ppermute x10, starting transfers between devices, passed_along(): lax.ppermute(shard, axis, [(i, (i + by) % peers) for i in range(peers)])  17.1 us
    scatter-add x4, other arithmetic, retract(): return own.at[bound[0]].add(from_prev).at[bound[1]].add(from_next)  5.86 us
    dot_general x2, matrix products, local(): lax.dot_general(adj, dagg, (((0,), (0,)), ((), ())), preferred_element_ty...  4.17 us
    dot_general x2, matrix products, local(): lax.dot_general(s_act, dz_val, (((0,), (0,)), ((), ())), preferred_elemen...  4.05 us
  transfers between devices with their start and end apart: 11, of which 6 were waited for; matrix products, arithmetic and copies ran while one was open for 11% of the time, Pallas kernels for 0%

commit v1 on v0

v1 whole, which is shorter than its diff:
```python
import functools
import math

import jax
import jax.numpy as jnp
from jax import lax
from jax.experimental import pallas as pl
from jax.experimental.pallas import tpu as pltpu
from jax.sharding import PartitionSpec as P

ALPHA = 0.1
BF = jnp.bfloat16
F32 = jnp.float32
PARTS = 2


def dot(a, b):
    return jnp.dot(a, b, preferred_element_type=F32)


def kernel(
    sizes,
    hand, init_h, cot, slots, ew, bnd, w_h,
    sec_out, in_grad, wg_out,
    x0, ct, init, w, wt, adj_o, adj_b, adjt_o, adjt_b, oh, oht,
    agg, s_act, s_t, slope, x1, x2, dz, dagg, own, gin,
    gsend, grecv, bsend, brecv,
    keep, asend, arecv, ysend, yrecv, tkeep, zsend, zrecv, wg,
    loc_sem, hs, hr, gs, gr, bs, br, a_s, a_r, y_s, y_r, z_s, z_r, q_s, q_r, f_s, f_r, e_s, e_r,
):
    npipe, ndom, nrep, rows, feat, width, layers = sizes
    nz = ndom // 2
    prow = feat // ndom
    half = feat // PARTS
    quart = half // nrep
    rb = 128
    blocks = rows // rb
    scale = 1.0 / math.sqrt(rows * ndom * nrep)

    pipe = lax.axis_index("pipe")
    dom = lax.axis_index("dom")
    rep = lax.axis_index("rep")
    z = dom // 2
    y = dom % 2

    def dev(p=pipe, d=dom, r=rep):
        return (p, d, r)

    pipe_next = dev(p=(pipe + 1) % npipe)
    pipe_prev = dev(p=(pipe + npipe - 1) % npipe)
    dom_next = dev(d=(dom + 1) % ndom)
    dom_prev = dev(d=(dom + ndom - 1) % ndom)
    twin = dev(d=z * 2 + (1 - y))
    mate = dev(r=1 - rep)
    z_peers = [dev(d=((z + k) % nz) * 2 + y) for k in range(1, nz)]

    def remote(src, dst, ss, rs, to):
        return pltpu.make_async_remote_copy(
            src_ref=src, dst_ref=dst, send_sem=ss, recv_sem=rs,
            device_id=to, device_id_type=pl.DeviceIdType.MESH,
        )

    barrier = pltpu.get_barrier_semaphore()
    greeted = [pipe_next, pipe_prev, dom_next, dom_prev, twin, mate] + z_peers
    for peer in greeted:
        pl.semaphore_signal(barrier, inc=1, device_id=peer, device_id_type=pl.DeviceIdType.MESH)
    load_w = pltpu.make_async_copy(w_h, w, loc_sem.at[0])
    load_i = pltpu.make_async_copy(init_h, init, loc_sem.at[1])
    load_w.start()
    load_i.start()
    pl.semaphore_wait(barrier, len(greeted))

    sends = []

    def go(copy):
        copy.start()
        sends.append(copy)
        return copy

    def cols(c):
        return pl.ds(c * half, half)

    hand_c = [
        go(remote(hand.at[:, cols(c)], x0.at[:, cols(c)], hs.at[0, c], hr.at[0, c], pipe_next))
        for c in range(PARTS)
    ]
    cot_c = [
        go(remote(cot.at[:, cols(c)], ct.at[:, cols(c)], hs.at[1, c], hr.at[1, c], pipe_prev))
        for c in range(PARTS)
    ]

    def loop(fn, n=blocks):
        def step(i, carry):
            fn(pl.ds(pl.multiple_of(i * rb, rb), rb))
            return carry
        lax.fori_loop(0, n, step, 0)

    betas = []
    for layer in range(layers):
        value = jnp.float32(0.0)
        for seg in range(npipe):
            value = jnp.where(
                pipe == seg, jnp.float32(math.log(0.5 / (seg * layers + layer + 1) + 1.0)), value
            )
        betas.append(value)

    def build(i, carry):
        rr = pl.ds(pl.multiple_of(i * 16, 16), 16)
        slot = slots[rr, :]
        wide = ew[rr, :].astype(F32)
        bslot = jnp.where(slot < width, slot, jnp.where(slot >= width + rows, slot - rows, -1))
        oslot = slot - width
        col_o = lax.broadcasted_iota(jnp.int32, (16, rows), 1)
        col_b = lax.broadcasted_iota(jnp.int32, (16, 2 * width), 1)
        tot_o = jnp.zeros((16, rows), F32)
        tot_b = jnp.zeros((16, 2 * width), F32)
        for k in range(slots.shape[1]):
            wk = wide[:, k : k + 1]
            tot_o = tot_o + jnp.where(oslot[:, k : k + 1] == col_o, wk, 0.0)
            tot_b = tot_b + jnp.where(bslot[:, k : k + 1] == col_b, wk, 0.0)
        adj_o[rr, :] = tot_o.astype(BF)
        adj_b[rr, :] = tot_b.astype(BF)
        return carry

    ids = jnp.concatenate([bnd[0:1, :], bnd[1:2, :]], axis=1)
    oht[...] = jnp.where(
        lax.broadcasted_iota(jnp.int32, (rows, 2 * width), 0) == ids, 1.0, 0.0
    ).astype(BF)
    oh[...] = oht[...].T
    lax.fori_loop(0, rows // 16, build, 0)
    adjt_o[...] = adj_o[...].T
    adjt_b[...] = adj_b[...].T
    load_w.wait()
    load_i.wait()
    for layer in range(layers):
        wt[layer] = w[layer].T

    lo, hi = pl.ds(0, width), pl.ds(width, width)

    def swap(send, recv, layer, cc, ss, rs, n):
        first = go(remote(send.at[layer, lo, cc], recv.at[layer, hi, cc], ss.at[n, 0], rs.at[n, 0], dom_prev))
        second = go(remote(send.at[layer, hi, cc], recv.at[layer, lo, cc], ss.at[n, 1], rs.at[n, 1], dom_next))
        return first, second

    def gather(x, layer, cc, n):
        gsend[layer, :, cc] = dot(oh[...], x[:, cc]).astype(BF)
        return swap(gsend, grecv, layer, cc, gs, gr, n)

    def agg_own(x, cc):
        def body(rr):
            agg[rr, cc] = dot(adj_o[rr, :], x[:, cc])
        loop(body)

    def agg_end(layer, cc):
        def body(rr):
            total = agg[rr, cc] + dot(adj_b[rr, :], grecv[layer, :, cc])
            s_act[layer, rr, cc] = (
                (1.0 - ALPHA) * total + ALPHA * init[rr, cc].astype(F32)
            ).astype(BF)
        loop(body)

    def mix(layer, out):
        beta = betas[layer]

        def body(rr):
            s = s_act[layer, rr, :]
            value = (1.0 - beta) * s.astype(F32) + beta * dot(s, w[layer])
            sig = jax.nn.sigmoid(value)
            out[rr, :] = (value * sig).astype(BF)
            slope[layer, rr, :] = sig * (1.0 + value * (1.0 - sig))
        loop(body)

    every = pl.ds(0, feat)
    for c in range(PARTS):
        hand_c[c].wait_recv()
        pair = gather(x0, 0, cols(c), c)
        agg_own(x0, cols(c))
        for copy in pair:
            copy.wait_recv()
        agg_end(0, cols(c))
    mix(0, x1)
    pair = gather(x1, 1, every, PARTS)
    agg_own(x1, every)
    s_t[0] = s_act[0].T
    for copy in pair:
        copy.wait_recv()
    agg_end(1, every)
    mix(1, x2)
    out_1 = pltpu.make_async_copy(x2, sec_out, loc_sem.at[2])
    out_1.start()
    s_t[1] = s_act[1].T

    def unit(layer, c):
        return (layers - 1 - layer) * PARTS + c

    def mine(c):
        return pl.ds(pl.multiple_of(c * half + rep * quart, quart), quart)

    def piece(zz, yy):
        return pl.ds(pl.multiple_of((zz * 2 + yy) * prow, prow), prow)

    live = {}

    def ar_a(layer, c):
        u = unit(layer, c)

        def body(rr):
            value = dot(s_t[layer, rr, :], dz[layer, :, cols(c)])
            left, right = value[:, :quart], value[:, quart:]
            keep[u, rr, :] = jnp.where(rep == 0, left, right)
            asend[u, rr, :] = jnp.where(rep == 0, right, left).astype(BF)
        loop(body, feat // rb)
        live["a", u] = go(remote(asend.at[u], arecv.at[u], a_s.at[u], a_r.at[u], mate))

    def ar_y(layer, c):
        u = unit(layer, c)
        live["a", u].wait_recv()
        for zz in range(nz):
            pp = piece(zz, 1 - y)
            ysend[u, zz] = (keep[u, pp, :] + arecv[u, pp, :].astype(F32)).astype(BF)
        live["y", u] = go(remote(ysend.at[u], yrecv.at[u], y_s.at[u], y_r.at[u], twin))
        for zz in range(nz):
            pp = piece(zz, y)
            tkeep[u, zz] = keep[u, pp, :] + arecv[u, pp, :].astype(F32)

    def ar_z(layer, c):
        u = unit(layer, c)
        live["y", u].wait_recv()
        live["z", u] = []
        for k in range(1, nz):
            zz = (z + k) % nz
            zsend[u, k - 1] = (tkeep[u, zz] + yrecv[u, zz].astype(F32)).astype(BF)
            live["z", u].append(
                go(remote(zsend.at[u, k - 1], zrecv.at[u, k - 1], z_s.at[u, k - 1], z_r.at[u, k - 1], z_peers[k - 1]))
            )

    def ar_g(layer, c):
        u = unit(layer, c)
        total = tkeep[u, z] + yrecv[u, z].astype(F32)
        for k in range(1, nz):
            live["z", u][k - 1].wait_recv()
            total = total + zrecv[u, k - 1].astype(F32)
        wg[layer, z, y, :, mine(c)] = (betas[layer] * scale * total).astype(BF)
        spot = wg.at[layer, z, y, :, mine(c)]
        live["q", u] = [
            go(remote(spot, spot, q_s.at[u, k], q_r.at[u, k], z_peers[k])) for k in range(nz - 1)
        ]

    def ar_f(layer, c):
        u = unit(layer, c)
        for copy in live["q", u]:
            copy.wait_recv()
        spot = wg.at[layer, :, y, :, mine(c)]
        live["f", u] = go(remote(spot, spot, f_s.at[u], f_r.at[u], twin))

    def ar_e(layer, c):
        u = unit(layer, c)
        live["f", u].wait_recv()
        spot = wg.at[layer, :, :, :, mine(c)]
        live["e", u] = go(remote(spot, spot, e_s.at[u], e_r.at[u], mate))

    def ar_end(layer, c):
        live["e", unit(layer, c)].wait_recv()

    def back(layer):
        beta = betas[layer]

        def body(rr):
            d = dz[layer, rr, :]
            ds_val = (1.0 - beta) * d.astype(F32) + beta * dot(d, wt[layer])
            dagg[layer, rr, :] = ((1.0 - ALPHA) * ds_val).astype(BF)
        loop(body)
        bsend[layer] = dot(adjt_b[...], dagg[layer]).astype(BF)
        return swap(bsend, brecv, layer, every, bs, br, layer)

    def dext_own(layer):
        def body(rr):
            own[rr, :] = dot(adjt_o[rr, :], dagg[layer])
        loop(body)

    last = layers - 1
    for c in range(PARTS):
        cot_c[c].wait_recv()

        def scaled(rr):
            dz[last, rr, cols(c)] = (ct[rr, cols(c)].astype(F32) * slope[last, rr, cols(c)]).astype(BF)
        loop(scaled)
        if c < PARTS - 1:
            ar_a(last, c)
            ar_y(last, c)
            ar_z(last, c)
    pair = back(1)
    ar_a(1, 1)
    dext_own(1)
    ar_y(1, 1)
    for copy in pair:
        copy.wait_recv()

    def inner(rr):
        grad = (own[rr, :] + dot(oht[rr, :], brecv[1])).astype(BF)
        dz[0, rr, :] = (grad.astype(F32) * slope[0, rr, :]).astype(BF)
    loop(inner)
    ar_a(0, 0)
    ar_a(0, 1)
    ar_g(1, 0)
    ar_y(0, 0)
    ar_y(0, 1)
    ar_z(1, 1)
    pair = back(0)
    ar_z(0, 0)
    ar_z(0, 1)
    ar_f(1, 0)
    dext_own(0)
    ar_g(1, 1)
    for copy in pair:
        copy.wait_recv()

    def final(rr):
        gin[rr, :] = (own[rr, :] + dot(oht[rr, :], brecv[0])).astype(BF)
    ar_g(0, 0)
    ar_g(0, 1)
    ar_f(1, 1)
    loop(final)
    out_2 = pltpu.make_async_copy(gin, in_grad, loc_sem.at[3])
    out_2.start()
    ar_e(1, 0)
    ar_f(0, 0)
    ar_f(0, 1)
    ar_e(1, 1)
    ar_e(0, 0)
    ar_e(0, 1)
    ar_end(1, 0)
    ar_end(1, 1)
    ar_end(0, 0)
    ar_end(0, 1)
    out_3 = pltpu.make_async_copy(wg, wg_out, loc_sem.at[4])
    out_3.start()
    for copy in sends:
        copy.wait_send()
    out_1.wait()
    out_2.wait()
    out_3.wait()


def local(sizes, handoff, initial, cotangent, slots, edge_weight, boundary, weights):
    npipe, ndom, nrep, rows, feat, width, layers = sizes
    nz = ndom // 2
    prow = feat // ndom
    quart = feat // PARTS // nrep
    units = layers * PARTS
    sem = pltpu.SemaphoreType.DMA
    vm = pltpu.VMEM
    square = (rows, feat)
    scratch = [
        vm(square, BF), vm(square, BF), vm(square, BF),
        vm((layers, feat, feat), BF), vm((layers, feat, feat), BF),
        vm((rows, rows), BF), vm((rows, 2 * width), BF),
        vm((rows, rows), BF), vm((2 * width, rows), BF),
        vm((2 * width, rows), BF), vm((rows, 2 * width), BF),
        vm(square, F32), vm((layers, rows, feat), BF), vm((layers, feat, rows), BF),
        vm((layers, rows, feat), F32), vm(square, BF), vm(square, BF),
        vm((layers, rows, feat), BF), vm((layers, rows, feat), BF), vm(square, F32), vm(square, BF),
        vm((layers, 2 * width, feat), BF), vm((layers, 2 * width, feat), BF),
        vm((layers, 2 * width, feat), BF), vm((layers, 2 * width, feat), BF),
        vm((units, feat, quart), F32), vm((units, feat, quart), BF), vm((units, feat, quart), BF),
        vm((units, nz, prow, quart), BF), vm((units, nz, prow, quart), BF),
        vm((units, nz, prow, quart), F32),
        vm((units, nz - 1, prow, quart), BF), vm((units, nz - 1, prow, quart), BF),
        vm((layers, nz, 2, prow, feat), BF),
        sem((5,)), sem((2, PARTS)), sem((2, PARTS)),
        sem((PARTS + 1, 2)), sem((PARTS + 1, 2)), sem((layers, 2)), sem((layers, 2)),
        sem((units,)), sem((units,)), sem((units,)), sem((units,)),
        sem((units, nz - 1)), sem((units, nz - 1)), sem((units, nz - 1)), sem((units, nz - 1)),
        sem((units,)), sem((units,)), sem((units,)), sem((units,)),
    ]
    anywhere = pl.BlockSpec(memory_space=pl.ANY)
    inside = pl.BlockSpec(memory_space=pltpu.VMEM)
    out, grad, wg = pl.pallas_call(
        functools.partial(kernel, sizes),
        out_shape=(
            jax.ShapeDtypeStruct(square, BF),
            jax.ShapeDtypeStruct(square, BF),
            jax.ShapeDtypeStruct((layers, nz, 2, prow, feat), BF),
        ),
        in_specs=[anywhere, anywhere, anywhere, inside, inside, inside, anywhere],
        out_specs=(anywhere, anywhere, anywhere),
        scratch_shapes=scratch,
        compiler_params=pltpu.CompilerParams(
            collective_id=0, has_side_effects=True, vmem_limit_bytes=48 * 1024 * 1024
        ),
        name="relay",
    )(
        handoff[0, 0], initial[0, 0], cotangent[0, 0], slots[0, 0], edge_weight[0, 0],
        boundary[0, 0, 0], weights,
    )
    return out[None, None], grad[None, None], wg.reshape(layers, feat, feat)


def solution(mesh):
    shape = dict(mesh.shape)
    specs = P("pipe", "rep", "dom", None)

    def whole(handoff, initial, cotangent, slots, edge_weight, boundary, weights):
        sizes = (
            shape["pipe"], shape["dom"], shape["rep"],
            handoff.shape[2] // shape["dom"], handoff.shape[3],
            boundary.shape[-1], weights.shape[0] // shape["pipe"],
        )
        return jax.shard_map(
            functools.partial(local, sizes),
            mesh=mesh,
            in_specs=(specs,) * 5 + (P("pipe", "rep", "dom", None, None), P("pipe", None, None)),
            out_specs=(specs, specs, P("pipe", None, None)),
            check_vma=False,
        )(handoff, initial, cotangent, slots, edge_weight, boundary, weights)

    return whole
```

time: 188 us -> 76.5 us (0.41)
  waiting for transfers between devices: 120 us -> 0 us
  Pallas kernels: 0 us -> 66.9 us
  starting transfers between devices: 17.1 us -> 0 us
  other arithmetic: 14.7 us -> 0 us
  between operations: 14.5 us -> 0.68 us
  matrix products: 13.1 us -> 0 us
  local copies, waits for them, and re-layouts: 6.55 us -> 8.55 us
    psum x1 -> x0, waiting for transfers between devices: 89.1 us -> none  [local(): summed = lax.psum(term, ('dom', 'rep'))]
    pallas_call x0 -> x1, Pallas kernels: none -> 66.9 us  [local(): pl.pallas_call(functools.partial(kernel, sizes), out_shape=(jax.ShapeDtyp...]
    ppermute x10 -> x0, waiting for transfers between devices: 30.9 us -> none  [passed_along(): lax.ppermute(shard, axis, [(i, (i + by) % peers) for i in range(peers)])]
    ppermute x10 -> x0, starting transfers between devices: 17.1 us -> none  [passed_along(): lax.ppermute(shard, axis, [(i, (i + by) % peers) for i in range(peers)])]
    dot_general x8 -> x0, matrix products: 13.1 us -> none  [the longest x2 4.17 us: local(): lax.dot_general(adj, dagg, (((0,), (0,)), ((), ())), preferred_element_ty...]
    unnamed x18 -> x17, local copies, waits for them, and re-layouts: 1.87 us -> 8.55 us
    scatter-add x4 -> x0, other arithmetic: 5.86 us -> none  [retract(): return own.at[bound[0]].add(from_prev).at[bound[1]].add(from_next)]
    convert_element_type x2 -> x0, other arithmetic: 3.33 us -> none  [the longest x1 2.94 us: adjacency(): return total.astype(jnp.bfloat16)]
  transfers between devices with their start and end apart: 11 -> 0, of which waited for: 6 -> 0; matrix products, arithmetic and copies ran while one was open for 11% -> 0% of each run, Pallas kernels for 0% -> 0%
where the time goes in v1:
time: 76.5 us; the launch traced here: 76.1 us
  Pallas kernels  66.9 us (87%)
  local copies, waits for them, and re-layouts  8.55 us (11%)
    pallas_call x1, Pallas kernels, local(): pl.pallas_call(functools.partial(kernel, sizes), out_shape=(jax.ShapeDtyp...  66.9 us
    unnamed x17, local copies, waits for them, and re-layouts  8.55 us

profile of v1, /device:TPU:1, one launch (start us, length us, event | category | flops | bytes accessed | tf_op | source)
XLA Modules:
  0.0 76.1 jit_solution(11682713227808139525)
XLA Ops:
  0.6 0.0 copy-start.5
  0.6 0.8 %copy.11 = bf16[1,1,512,16]{3,2,1,0:T(8,128)(2,1)S(1)} copy(bf16[1,1,512,16]{2,3,1,0:T(8,128)(2,1)} %param.11) | data formatting | bytes 32768 | tf_op args[4]
  1.5 0.0 copy-done.5
  1.5 0.1 copy.10
  1.6 0.0 copy-start.4
  1.6 0.7 copy-done.4
  2.3 0.0 copy-start
  2.3 1.2 %copy-done = bf16[2,512,512]{2,1,0:T(8,128)(2,1)S(1)} copy-done((bf16[2,512,512]{2,1,0:T(8,128)(2,1)S(1)}, bf16[2,512,512]{2,1,0:T(8,128)(2,1)}, u32[]{:S(2)}) %copy-start) | copy-done | bytes 1048600
  3.5 0.0 copy-start.1
  3.5 1.0 %copy-done.1 = bf16[1,1,512,512]{3,2,1,0:T(8,128)(2,1)S(1)} copy-done((bf16[1,1,512,512]{3,2,1,0:T(8,128)(2,1)S(1)}, bf16[1,1,512,512]{3,2,1,0:T(8,128)(2,1)}, u32[]{:S(2)}) %copy-start.1) | copy-done | bytes 524312
  4.6 0.0 copy-start.2
  4.6 1.0 %copy-done.2 = bf16[1,1,512,512]{3,2,1,0:T(8,128)(2,1)S(1)} copy-done((bf16[1,1,512,512]{3,2,1,0:T(8,128)(2,1)S(1)}, bf16[1,1,512,512]{3,2,1,0:T(8,128)(2,1)}, u32[]{:S(2)}) %copy-start.2) | copy-done | bytes 524312
  5.6 0.0 copy-start.3
  5.6 1.0 %copy-done.3 = bf16[1,1,512,512]{3,2,1,0:T(8,128)(2,1)S(1)} copy-done((bf16[1,1,512,512]{3,2,1,0:T(8,128)(2,1)S(1)}, bf16[1,1,512,512]{3,2,1,0:T(8,128)(2,1)}, u32[]{:S(2)}) %copy-start.3) | copy-done | bytes 524312
  6.7 66.9 %relay.1 = (bf16[512,512]{1,0:T(8,128)(2,1)S(1)}, bf16[512,512]{1,0:T(8,128)(2,1)S(1)}, bf16[2,4,2,64,512]{4,3,2,1,0:T(8,128)(2,1)S(1)}) custom-call(bf16[512,512]{1,0:T(8,128)(2,1)S(1)} %bitcast.14, bf16[512,512]{1,0:T(8,128)(2,1)S(1)} %bitcast.15, bf16[512,512]{1,0:T(8,128)(2,1)S(1)} %bitcast.16, s32[512,16]{1,0:T(8,128)S(1)} %bitcast.10, ...), custom_call_target="tpu_custom_call" | custom-call | tf_op jit(solution)/shard_map/relay/pallas_call | solution.py:378
  73.6 0.8 %copy.15 = bf16[1,1,512,512]{3,2,1,0:T(8,128)(2,1)} copy(bf16[1,1,512,512]{3,2,1,0:T(8,128)(2,1)S(1)} %bitcast.13) | data formatting | bytes 1048576
  74.4 0.8 %copy.16 = bf16[1,1,512,512]{3,2,1,0:T(8,128)(2,1)} copy(bf16[1,1,512,512]{3,2,1,0:T(8,128)(2,1)S(1)} %bitcast.12) | data formatting | bytes 1048576
  75.2 1.0 %copy.17 = bf16[2,512,512]{2,1,0:T(8,128)(2,1)} copy(bf16[2,512,512]{2,1,0:T(8,128)(2,1)S(1)} %bitcast.9) | data formatting | bytes 2097152
Async XLA Ops:
  0.6 0.9 %copy-start.5 = (s32[1,1,512,16]{2,3,1,0:T(8,128)S(1)}, s32[1,1,512,16]{2,3,1,0:T(8,128)}, u32[]{:S(2)}) copy-start(s32[1,1,512,16]{2,3,1,0:T(8,128)} %param.10) | copy-start | bytes 98308
  1.6 0.7 copy-start.4
  2.3 1.2 %copy-start = (bf16[2,512,512]{2,1,0:T(8,128)(2,1)S(1)}, bf16[2,512,512]{2,1,0:T(8,128)(2,1)}, u32[]{:S(2)}) copy-start(bf16[2,512,512]{2,1,0:T(8,128)(2,1)} %w_h.1) | copy-start | bytes 3145732
  3.5 1.0 %copy-start.1 = (bf16[1,1,512,512]{3,2,1,0:T(8,128)(2,1)S(1)}, bf16[1,1,512,512]{3,2,1,0:T(8,128)(2,1)}, u32[]{:S(2)}) copy-start(bf16[1,1,512,512]{3,2,1,0:T(8,128)(2,1)} %param.7) | copy-start | bytes 1572868
  4.6 1.0 %copy-start.2 = (bf16[1,1,512,512]{3,2,1,0:T(8,128)(2,1)S(1)}, bf16[1,1,512,512]{3,2,1,0:T(8,128)(2,1)}, u32[]{:S(2)}) copy-start(bf16[1,1,512,512]{3,2,1,0:T(8,128)(2,1)} %param.8) | copy-start | bytes 1572868
  5.6 1.0 %copy-start.3 = (bf16[1,1,512,512]{3,2,1,0:T(8,128)(2,1)S(1)}, bf16[1,1,512,512]{3,2,1,0:T(8,128)(2,1)}, u32[]{:S(2)}) copy-start(bf16[1,1,512,512]{3,2,1,0:T(8,128)(2,1)} %param.9) | copy-start | bytes 1572868

commit v2 on v1

--- a/solution.py
+++ b/solution.py
@@ -1,3 +1,4 @@
+import contextlib
 import functools
 import math
 
@@ -18,14 +19,20 @@
     return jnp.dot(a, b, preferred_element_type=F32)
 
 
+def scope(name):
+    return contextlib.nullcontext()
+
+
 def kernel(
     sizes,
-    hand, init_h, cot, slots, ew, bnd, w_h,
+    hand, init_h, cot, slots_h, ew_h, bnd_h, w_h,
     sec_out, in_grad, wg_out,
+    x2, gin, wg,
+    slots, ew, bnd,
     x0, ct, init, w, wt, adj_o, adj_b, adjt_o, adjt_b, oh, oht,
-    agg, s_act, s_t, slope, x1, x2, dz, dagg, own, gin,
+    agg, s_act, s_t, slope, x1, dz, dagg, own,
     gsend, grecv, bsend, brecv,
-    keep, asend, arecv, ysend, yrecv, tkeep, zsend, zrecv, wg,
+    keep, asend, arecv, ysend, yrecv, tkeep, zsend, zrecv,
     loc_sem, hs, hr, gs, gr, bs, br, a_s, a_r, y_s, y_r, z_s, z_r, q_s, q_r, f_s, f_r, e_s, e_r,
 ):
     npipe, ndom, nrep, rows, feat, width, layers = sizes
@@ -66,6 +73,12 @@
         pl.semaphore_signal(barrier, inc=1, device_id=peer, device_id_type=pl.DeviceIdType.MESH)
     load_w = pltpu.make_async_copy(w_h, w, loc_sem.at[0])
     load_i = pltpu.make_async_copy(init_h, init, loc_sem.at[1])
+    loads = [
+        pltpu.make_async_copy(src, dst, loc_sem.at[2 + i])
+        for i, (src, dst) in enumerate(((bnd_h, bnd), (slots_h, slots), (ew_h, ew)))
+    ]
+    for copy in loads:
+        copy.start()
     load_w.start()
     load_i.start()
     pl.semaphore_wait(barrier, len(greeted))
@@ -104,32 +117,30 @@
             )
         betas.append(value)
 
-    def build(i, carry):
-        rr = pl.ds(pl.multiple_of(i * 16, 16), 16)
-        slot = slots[rr, :]
-        wide = ew[rr, :].astype(F32)
-        bslot = jnp.where(slot < width, slot, jnp.where(slot >= width + rows, slot - rows, -1))
-        oslot = slot - width
-        col_o = lax.broadcasted_iota(jnp.int32, (16, rows), 1)
-        col_b = lax.broadcasted_iota(jnp.int32, (16, 2 * width), 1)
-        tot_o = jnp.zeros((16, rows), F32)
-        tot_b = jnp.zeros((16, 2 * width), F32)
-        for k in range(slots.shape[1]):
-            wk = wide[:, k : k + 1]
-            tot_o = tot_o + jnp.where(oslot[:, k : k + 1] == col_o, wk, 0.0)
-            tot_b = tot_b + jnp.where(bslot[:, k : k + 1] == col_b, wk, 0.0)
-        adj_o[rr, :] = tot_o.astype(BF)
-        adj_b[rr, :] = tot_b.astype(BF)
-        return carry
-
-    ids = jnp.concatenate([bnd[0:1, :], bnd[1:2, :]], axis=1)
-    oht[...] = jnp.where(
-        lax.broadcasted_iota(jnp.int32, (rows, 2 * width), 0) == ids, 1.0, 0.0
-    ).astype(BF)
-    oh[...] = oht[...].T
-    lax.fori_loop(0, rows // 16, build, 0)
-    adjt_o[...] = adj_o[...].T
-    adjt_b[...] = adj_b[...].T
+    def build(target, first):
+        def body(i, carry):
+            jj = pl.multiple_of(i * 16, 16)
+            col = lax.broadcasted_iota(jnp.int32, (16, rows), 0) + first(jj)
+            total = jnp.zeros((16, rows), F32)
+            for k in range(slots.shape[0]):
+                weight = ew[k : k + 1, :].astype(F32)
+                total = total + jnp.where(slots[k : k + 1, :] == col, weight, 0.0)
+            target[pl.ds(jj, 16), :] = total.astype(BF)
+            return carry
+        lax.fori_loop(0, target.shape[0] // 16, body, 0)
+
+    for copy in loads:
+        copy.wait()
+    with scope("build"):
+        ids = jnp.concatenate([bnd[0:1, :], bnd[1:2, :]], axis=1)
+        oht[...] = jnp.where(
+            lax.broadcasted_iota(jnp.int32, (rows, 2 * width), 0) == ids, 1.0, 0.0
+        ).astype(BF)
+        oh[...] = oht[...].T
+        build(adjt_o, lambda jj: jj + width)
+        build(adjt_b, lambda jj: jnp.where(jj < width, jj, jj + rows))
+        adj_o[...] = adjt_o[...].T
+        adj_b[...] = adjt_b[...].T
     load_w.wait()
     load_i.wait()
     for layer in range(layers):
@@ -186,7 +197,7 @@
         copy.wait_recv()
     agg_end(1, every)
     mix(1, x2)
-    out_1 = pltpu.make_async_copy(x2, sec_out, loc_sem.at[2])
+    out_1 = pltpu.make_async_copy(x2, sec_out, loc_sem.at[5])
     out_1.start()
     s_t[1] = s_act[1].T
 
@@ -287,10 +298,9 @@
         loop(scaled)
         if c < PARTS - 1:
             ar_a(last, c)
-            ar_y(last, c)
-            ar_z(last, c)
     pair = back(1)
     ar_a(1, 1)
+    ar_y(1, 0)
     dext_own(1)
     ar_y(1, 1)
     for copy in pair:
@@ -302,16 +312,18 @@
     loop(inner)
     ar_a(0, 0)
     ar_a(0, 1)
+    ar_z(1, 0)
+    ar_y(0, 0)
+    ar_z(1, 1)
+    ar_y(0, 1)
+    pair = back(0)
     ar_g(1, 0)
-    ar_y(0, 0)
-    ar_y(0, 1)
-    ar_z(1, 1)
-    pair = back(0)
+    ar_g(1, 1)
     ar_z(0, 0)
+    dext_own(0)
     ar_z(0, 1)
     ar_f(1, 0)
-    dext_own(0)
-    ar_g(1, 1)
+    ar_f(1, 1)
     for copy in pair:
         copy.wait_recv()
 
@@ -319,27 +331,41 @@
         gin[rr, :] = (own[rr, :] + dot(oht[rr, :], brecv[0])).astype(BF)
     ar_g(0, 0)
     ar_g(0, 1)
-    ar_f(1, 1)
     loop(final)
-    out_2 = pltpu.make_async_copy(gin, in_grad, loc_sem.at[3])
+    out_2 = pltpu.make_async_copy(gin, in_grad, loc_sem.at[6])
     out_2.start()
     ar_e(1, 0)
+    ar_e(1, 1)
     ar_f(0, 0)
     ar_f(0, 1)
-    ar_e(1, 1)
+    ar_end(1, 0)
+    ar_end(1, 1)
+    out_3 = pltpu.make_async_copy(wg.at[1], wg_out.at[1], loc_sem.at[7])
+    out_3.start()
     ar_e(0, 0)
     ar_e(0, 1)
-    ar_end(1, 0)
-    ar_end(1, 1)
     ar_end(0, 0)
     ar_end(0, 1)
-    out_3 = pltpu.make_async_copy(wg, wg_out, loc_sem.at[4])
-    out_3.start()
+    out_4 = pltpu.make_async_copy(wg.at[0], wg_out.at[0], loc_sem.at[8])
+    out_4.start()
+    for copy in (out_1, out_2, out_3, out_4):
+        copy.wait()
     for copy in sends:
         copy.wait_send()
-    out_1.wait()
-    out_2.wait()
-    out_3.wait()
+
+
+def put_out(a, b, c, a_out, b_out, c_out, a_mid, b_mid, c_mid, sems):
+    loads, stores = [], []
+    for i, (src, mid, dst) in enumerate(((a, a_mid, a_out), (b, b_mid, b_out), (c, c_mid, c_out))):
+        loads.append(pltpu.make_async_copy(src, mid, sems.at[0, i]))
+        stores.append(pltpu.make_async_copy(mid, dst, sems.at[1, i]))
+    for load in loads:
+        load.start()
+    for load, store in zip(loads, stores):
+        load.wait()
+        store.start()
+    for store in stores:
+        store.wait()
 
 
 def local(sizes, handoff, initial, cotangent, slots, edge_weight, boundary, weights):
@@ -351,48 +377,59 @@
     sem = pltpu.SemaphoreType.DMA
     vm = pltpu.VMEM
     square = (rows, feat)
+    taps = slots.shape[-1]
     scratch = [
+        vm(square, BF), vm(square, BF), vm((layers, nz, 2, prow, feat), BF),
+        vm((taps, rows), jnp.int32), vm((taps, rows), BF), vm((2, width), jnp.int32),
         vm(square, BF), vm(square, BF), vm(square, BF),
         vm((layers, feat, feat), BF), vm((layers, feat, feat), BF),
         vm((rows, rows), BF), vm((rows, 2 * width), BF),
         vm((rows, rows), BF), vm((2 * width, rows), BF),
         vm((2 * width, rows), BF), vm((rows, 2 * width), BF),
         vm(square, F32), vm((layers, rows, feat), BF), vm((layers, feat, rows), BF),
-        vm((layers, rows, feat), F32), vm(square, BF), vm(square, BF),
-        vm((layers, rows, feat), BF), vm((layers, rows, feat), BF), vm(square, F32), vm(square, BF),
+        vm((layers, rows, feat), F32), vm(square, BF),
+        vm((layers, rows, feat), BF), vm((layers, rows, feat), BF), vm(square, F32),
         vm((layers, 2 * width, feat), BF), vm((layers, 2 * width, feat), BF),
         vm((layers, 2 * width, feat), BF), vm((layers, 2 * width, feat), BF),
         vm((units, feat, quart), F32), vm((units, feat, quart), BF), vm((units, feat, quart), BF),
         vm((units, nz, prow, quart), BF), vm((units, nz, prow, quart), BF),
         vm((units, nz, prow, quart), F32),
         vm((units, nz - 1, prow, quart), BF), vm((units, nz - 1, prow, quart), BF),
-        vm((layers, nz, 2, prow, feat), BF),
-        sem((5,)), sem((2, PARTS)), sem((2, PARTS)),
+        sem((9,)), sem((2, PARTS)), sem((2, PARTS)),
         sem((PARTS + 1, 2)), sem((PARTS + 1, 2)), sem((layers, 2)), sem((layers, 2)),
         sem((units,)), sem((units,)), sem((units,)), sem((units,)),
         sem((units, nz - 1)), sem((units, nz - 1)), sem((units, nz - 1)), sem((units, nz - 1)),
         sem((units,)), sem((units,)), sem((units,)), sem((units,)),
     ]
-    anywhere = pl.BlockSpec(memory_space=pl.ANY)
-    inside = pl.BlockSpec(memory_space=pltpu.VMEM)
-    out, grad, wg = pl.pallas_call(
+    far = pl.BlockSpec(memory_space=pltpu.HBM)
+    shapes = (
+        jax.ShapeDtypeStruct(square, BF),
+        jax.ShapeDtypeStruct(square, BF),
+        jax.ShapeDtypeStruct((layers, nz, 2, prow, feat), BF),
+    )
+    made = pl.pallas_call(
         functools.partial(kernel, sizes),
-        out_shape=(
-            jax.ShapeDtypeStruct(square, BF),
-            jax.ShapeDtypeStruct(square, BF),
-            jax.ShapeDtypeStruct((layers, nz, 2, prow, feat), BF),
-        ),
-        in_specs=[anywhere, anywhere, anywhere, inside, inside, inside, anywhere],
-        out_specs=(anywhere, anywhere, anywhere),
+        out_shape=shapes,
+        in_specs=[far] * 7,
+        out_specs=(far,) * 3,
         scratch_shapes=scratch,
         compiler_params=pltpu.CompilerParams(
-            collective_id=0, has_side_effects=True, vmem_limit_bytes=48 * 1024 * 1024
+            collective_id=0, has_side_effects=True, vmem_limit_bytes=60 * 1024 * 1024
         ),
         name="relay",
     )(
-        handoff[0, 0], initial[0, 0], cotangent[0, 0], slots[0, 0], edge_weight[0, 0],
+        handoff[0, 0], initial[0, 0], cotangent[0, 0], slots[0, 0].T, edge_weight[0, 0].T,
         boundary[0, 0, 0], weights,
     )
+    out, grad, wg = pl.pallas_call(
+        put_out,
+        out_shape=shapes,
+        in_specs=[far] * 3,
+        out_specs=(far,) * 3,
+        scratch_shapes=[vm(one.shape, BF) for one in shapes] + [sem((2, 3))],
+        compiler_params=pltpu.CompilerParams(vmem_limit_bytes=60 * 1024 * 1024),
+        name="put_out",
+    )(*made)
     return out[None, None], grad[None, None], wg.reshape(layers, feat, feat)
 
 

time: 76.5 us -> 67.2 us (0.88)
  local copies, waits for them, and re-layouts: 8.55 us -> 0 us
    unnamed x17 -> x0, local copies, waits for them, and re-layouts: 8.55 us -> none
    pallas_call x1 -> x2, Pallas kernels: 66.9 us -> 66.4 us  [the longest x1 63.8 us: local(): pl.pallas_call(functools.partial(kernel, sizes), out_shape=shapes, in_spe...]
where the time goes in v2:
time: 67.2 us; the launch traced here: 67.1 us
  Pallas kernels  66.4 us (99%)
    pallas_call x1, Pallas kernels, local(): pl.pallas_call(functools.partial(kernel, sizes), out_shape=shapes, in_spe...  63.8 us
    pallas_call x1, Pallas kernels, local(): pl.pallas_call(put_out, out_shape=shapes, in_specs=[far] * 3, out_specs=(...  2.57 us

profile of v2, /device:TPU:1, one launch (start us, length us, event | category | flops | bytes accessed | tf_op | source)
XLA Modules:
  0.0 67.1 jit_solution(2889637846845250695)
XLA Ops:
  0.6 63.8 %relay.1 = (bf16[512,512]{1,0:T(8,128)(2,1)}, bf16[512,512]{1,0:T(8,128)(2,1)}, bf16[2,4,2,64,512]{4,3,2,1,0:T(8,128)(2,1)}) custom-call(bf16[512,512]{1,0:T(8,128)(2,1)} %bitcast.13, bf16[512,512]{1,0:T(8,128)(2,1)} %bitcast.14, bf16[512,512]{1,0:T(8,128)(2,1)} %bitcast.15, s32[16,512]{1,0:T(8,128)} %bitcast.16, bf16[16,512]{1,0:T(8,128)(2,1)} %bitcast.17, ...), custom_call_target="tpu_custom_call" | custom-call | tf_op jit(solution)/shard_map/relay/pallas_call | solution.py:410
  64.5 2.6 %put_out.1 = (bf16[512,512]{1,0:T(8,128)(2,1)}, bf16[512,512]{1,0:T(8,128)(2,1)}, bf16[2,4,2,64,512]{4,3,2,1,0:T(8,128)(2,1)}) custom-call(bf16[512,512]{1,0:T(8,128)(2,1)} %get-tuple-element.9.a, bf16[512,512]{1,0:T(8,128)(2,1)} %get-tuple-element.10.b, bf16[2,4,2,64,512]{4,3,2,1,0:T(8,128)(2,1)} %get-tuple-element.11.c), custom_call_target="tpu_custom_call" | custom-call | tf_op jit(solution)/shard_map/put_out/pallas_call | solution.py:424
